TPU v7x, 128 devices: a whole 4x4x4 slice. The times are simulated.
128 devices in a mesh: obs: 8 (over z_hi, y), unk: 16 (over z_lo, x, core).
Axes of the slice: x: 4, y: 4, z: 4 (z_hi: 2, z_lo: 2; z = z_hi * 2 + z_lo), core: 2. Of those that a mesh axis runs over, the one named last changes fastest.
Arguments:
- design: float32 [8192, 24576], P('obs', 'unk'), may hold values from -0.0625 to 0.0625
- weights: float32 [8192], P('obs'), may hold values from 0.25 to 4
Outputs:
- factor: float32 [24576, 1024], P(('unk', 'obs'))
All inputs are finite; a program needn't handle non-finite values.
Results may differ from a plain program's by a relative error of at most 0.00011.
Values sent between devices are 32-bit elements; how exact they have to be, the bound alone decides.
No kernel may reach another device: no remote copies, remote signals or barrier semaphores. Data moves between devices by JAX's collectives and lax.ppermute only.
A program may use at most 128 MiB of HBM per device.

v0:
```python
import jax
import jax.numpy as jnp
from jax import lax
from jax.sharding import PartitionSpec as P

PANEL = 512
BLOCK = 128


def spread(block, axis, holder):
    block = jnp.where(lax.axis_index(axis) == holder, block, jnp.zeros_like(block))
    return lax.psum(block, axis)


def apply_lower(diag_factor, values):
    return lax.linalg.triangular_solve(
        diag_factor, values, left_side=False, lower=True, transpose_a=True
    )


def left_looking(top_block, owned_rows):
    width = top_block.shape[0]
    factor_top = jnp.zeros_like(top_block)
    factor_rows = jnp.zeros_like(owned_rows)
    for column_block in range(width // BLOCK):
        offset = column_block * BLOCK
        update_top = top_block[:, offset : offset + BLOCK]
        update_rows = owned_rows[:, offset : offset + BLOCK]
        if offset > 0:
            earlier = factor_top[offset : offset + BLOCK, :offset]
            update_top = update_top - jnp.dot(
                factor_top[:, :offset],
                earlier.T,
                precision=lax.Precision.HIGHEST,
                preferred_element_type=jnp.float32,
            )
            update_rows = update_rows - jnp.dot(
                factor_rows[:, :offset],
                earlier.T,
                precision=lax.Precision.HIGHEST,
                preferred_element_type=jnp.float32,
            )
        diag_factor = jnp.linalg.cholesky(update_top[offset : offset + BLOCK])
        below_top = apply_lower(diag_factor, update_top[offset + BLOCK :])
        new_column = jnp.concatenate(
            [jnp.zeros((offset, BLOCK), jnp.float32), diag_factor, below_top], axis=0
        )
        factor_top = factor_top.at[:, offset : offset + BLOCK].set(new_column)
        factor_rows = factor_rows.at[:, offset : offset + BLOCK].set(
            apply_lower(diag_factor, update_rows)
        )
    return factor_rows


def local(design, weights):
    panel_cols = spread(design[:, : 2 * PANEL], "unk", 0)
    weighted = panel_cols * weights[:, None]
    partial_value = lax.dot_general(
        design,
        weighted,
        (((0,), (0,)), ((), ())),
        precision=lax.Precision.HIGHEST,
        preferred_element_type=jnp.float32,
    )
    owned_rows = lax.psum_scatter(partial_value, "obs", scatter_dimension=0, tiled=True)
    gathered = lax.all_gather(owned_rows, "obs", axis=0, tiled=True)
    top_block = spread(gathered[: 2 * PANEL], "unk", 0)
    return left_looking(top_block, owned_rows)


def solution(mesh):
    return jax.shard_map(
        local,
        mesh=mesh,
        in_specs=(P("obs", "unk"), P("obs")),
        out_specs=P(("unk", "obs"), None),
        check_vma=False,
    )
```

profile of v0, /device:TPU:7, one launch (start us, length us, event | category | flops | bytes accessed | tf_op | source)
XLA Modules:
  0.0 775.2 jit_solution(10792649230344124611)
XLA Ops:
  6.5 4.7 slice.463
  11.3 5.3 copy.46
  19.5 132.4 %all-reduce.5.cloned.1.call-done = f32[1024,1024]{0,1:T(8,128)} async-done(((f32[1024,1024]{0,1:T(8,128)}), f32[1024,1024]{0,1:T(8,128)}) %all-reduce.5.cloned.1.call-update) | async-done | bytes 4194320 | tf_op jit(solution)/shard_map/psum | solution.py:12
  151.9 24.3 %convolution_bitcast_fusion = f32[1536,1024]{0,1:T(8,128)} fusion(f32[1024,1536]{1,0:T(8,128)} %param.35, f32[1024,1024]{0,1:T(8,128)} %all-reduce.5.cloned.1.call-done, f32[1024]{0:T(1024)S(1)} %copy-done.3), kind=kOutput, calls=%fused_computation | convolution fusion | flops 19328401408 | bytes 16781312 | tf_op jit(solution)/shard_map/dot_general | solution.py:58
  176.3 6.5 copy.44
  182.9 98.6 %reduce-scatter.4.cloned.1.call-done = f32[192,1024]{1,0:T(8,128)} async-done(((f32[1536,1024]{1,0:T(8,128)}), f32[192,1024]{1,0:T(8,128)}) %reduce-scatter.4.cloned.1.call-update) | async-done | bytes 786448 | tf_op jit(solution)/shard_map/reduce_scatter | solution.py:65
  281.5 90.1 %all-gather.2.cloned.1.call-done = f32[1536,1024]{1,0:T(8,128)} async-done(((f32[192,1024]{1,0:T(8,128)}), f32[1536,1024]{1,0:T(8,128)}) %all-gather.2.cloned.1.call-update) | async-done | bytes 6291472 | tf_op jit(solution)/shard_map/all_gather | solution.py:66
  371.6 4.7 slice.519
  376.3 5.3 copy.47
  381.7 2.8 broadcast_select_fusion
  390.4 122.7 %all-reduce.7.cloned.1.call-done = f32[1024,1024]{0,1:T(8,128)} async-done(((f32[1024,1024]{0,1:T(8,128)}), f32[1024,1024]{0,1:T(8,128)}) %all-reduce.7.cloned.1.call-update) | async-done | bytes 4194320 | tf_op jit(solution)/shard_map/psum | solution.py:12
  514.9 11.7 %cholesky.134 = f32[128,128]{1,0:T(8,128)S(1)} custom-call(f32[128,128]{1,0:T(8,128)S(1)} %fusion.101), custom_call_target="Cholesky" | custom-call | tf_op jit(solution)/shard_map/jit(cholesky)/cholesky | solution.py:43
  527.9 9.8 %custom-call.40 = f32[1,128,128]{1,2,0:T(8,128)S(1)} custom-call(f32[1,128,128]{2,1,0:T(8,128)S(1)} %get-tuple-element.199), custom_call_target="InvertDiagBlocksLowerTriangular" | custom-call | tf_op jit(solution)/shard_map/triangular_solve/custom-call.0 | solution.py:16
  545.2 11.9 %cholesky.145 = f32[128,128]{1,0:T(8,128)S(1)} custom-call(f32[128,128]{1,0:T(8,128)S(1)} %fusion.98), custom_call_target="Cholesky" | custom-call | tf_op jit(solution)/shard_map/jit(cholesky)/cholesky | solution.py:43
  558.4 9.8 %custom-call.41 = f32[1,128,128]{1,2,0:T(8,128)S(1)} custom-call(f32[1,128,128]{2,1,0:T(8,128)S(1)} %get-tuple-element.197), custom_call_target="InvertDiagBlocksLowerTriangular" | custom-call | tf_op jit(solution)/shard_map/triangular_solve/custom-call.0 | solution.py:16
  573.4 11.7 %cholesky.156 = f32[128,128]{1,0:T(8,128)S(1)} custom-call(f32[128,128]{1,0:T(8,128)S(1)} %fusion.95), custom_call_target="Cholesky" | custom-call | tf_op jit(solution)/shard_map/jit(cholesky)/cholesky | solution.py:43
  586.4 9.8 %custom-call.42 = f32[1,128,128]{1,2,0:T(8,128)S(1)} custom-call(f32[1,128,128]{2,1,0:T(8,128)S(1)} %get-tuple-element.195), custom_call_target="InvertDiagBlocksLowerTriangular" | custom-call | tf_op jit(solution)/shard_map/triangular_solve/custom-call.0 | solution.py:16
  603.1 3.4 fusion.15
  606.6 11.7 %cholesky.167 = f32[128,128]{1,0:T(8,128)S(1)} custom-call(f32[128,128]{1,0:T(8,128)S(1)} %fusion.92), custom_call_target="Cholesky" | custom-call | tf_op jit(solution)/shard_map/jit(cholesky)/cholesky | solution.py:43
  619.7 9.8 %custom-call.43 = f32[1,128,128]{1,2,0:T(8,128)S(1)} custom-call(f32[1,128,128]{2,1,0:T(8,128)S(1)} %get-tuple-element.193), custom_call_target="InvertDiagBlocksLowerTriangular" | custom-call | tf_op jit(solution)/shard_map/triangular_solve/custom-call.0 | solution.py:16
  635.3 4.0 fusion.21
  639.5 12.1 %cholesky.178 = f32[128,128]{1,0:T(8,128)S(1)} custom-call(f32[128,128]{1,0:T(8,128)S(1)} %fusion.89), custom_call_target="Cholesky" | custom-call | tf_op jit(solution)/shard_map/jit(cholesky)/cholesky | solution.py:43
  652.9 9.8 %custom-call.44 = f32[1,128,128]{1,2,0:T(8,128)S(1)} custom-call(f32[1,128,128]{2,1,0:T(8,128)S(1)} %get-tuple-element.191), custom_call_target="InvertDiagBlocksLowerTriangular" | custom-call | tf_op jit(solution)/shard_map/triangular_solve/custom-call.0 | solution.py:16
  668.3 4.7 fusion.18
  673.2 11.8 %cholesky.189 = f32[128,128]{1,0:T(8,128)S(1)} custom-call(f32[128,128]{1,0:T(8,128)S(1)} %fusion.86), custom_call_target="Cholesky" | custom-call | tf_op jit(solution)/shard_map/jit(cholesky)/cholesky | solution.py:43
  686.4 9.8 %custom-call.45 = f32[1,128,128]{1,2,0:T(8,128)S(1)} custom-call(f32[1,128,128]{2,1,0:T(8,128)S(1)} %get-tuple-element.189), custom_call_target="InvertDiagBlocksLowerTriangular" | custom-call | tf_op jit(solution)/shard_map/triangular_solve/custom-call.0 | solution.py:16
  702.0 5.4 fusion.12
  707.5 11.7 %cholesky.200 = f32[128,128]{1,0:T(8,128)S(1)} custom-call(f32[128,128]{1,0:T(8,128)S(1)} %fusion.83), custom_call_target="Cholesky" | custom-call | tf_op jit(solution)/shard_map/jit(cholesky)/cholesky | solution.py:43
  720.6 10.0 %custom-call.46 = f32[1,128,128]{1,2,0:T(8,128)S(1)} custom-call(f32[1,128,128]{2,1,0:T(8,128)S(1)} %get-tuple-element.187), custom_call_target="InvertDiagBlocksLowerTriangular" | custom-call | tf_op jit(solution)/shard_map/triangular_solve/custom-call.0 | solution.py:16
  736.3 6.0 fusion.1
  742.4 11.7 %cholesky.211 = f32[128,128]{1,0:T(8,128)S(1)} custom-call(f32[128,128]{1,0:T(8,128)S(1)} %fusion.80), custom_call_target="Cholesky" | custom-call | tf_op jit(solution)/shard_map/jit(cholesky)/cholesky | solution.py:43
  755.6 9.8 %custom-call.47 = f32[1,128,128]{1,2,0:T(8,128)S(1)} custom-call(f32[1,128,128]{2,1,0:T(8,128)S(1)} %fusion.76), custom_call_target="InvertDiagBlocksLowerTriangular" | custom-call | tf_op jit(solution)/shard_map/triangular_solve/custom-call.0 | solution.py:16
  (126 shorter events, 66.9 us)
Async XLA Ops:
  6.5 145.4 %all-reduce.5.cloned.1.call-start = ((), (), s32[]{:S(2)}) async-start(), calls=%async_computation.1 | async-start | bytes 8388608 | tf_op jit(solution)/shard_map/psum | solution.py:12
  19.4 132.5 %copy-start.3 = (f32[1024]{0:T(1024)S(1)}, f32[1024]{0:T(1024)}, u32[]{:S(2)}) copy-start(f32[1024]{0:T(1024)} %param.36) | copy-start | bytes 12292
  19.4 262.0 %reduce-scatter.4.cloned.1.call-start = ((), (), s32[]{:S(2)}) async-start(), calls=%async_computation.4 | async-start | bytes 7077888 | tf_op jit(solution)/shard_map/reduce_scatter | solution.py:65
  182.8 188.8 %all-gather.2.cloned.1.call-start = ((), (), s32[]{:S(2)}) async-start(), calls=%async_computation.2 | async-start | bytes 7077888 | tf_op jit(solution)/shard_map/all_gather | solution.py:66
  281.5 231.6 %all-reduce.7.cloned.1.call-start = ((), (), s32[]{:S(2)}) async-start(), calls=%async_computation.3 | async-start | bytes 8388608 | tf_op jit(solution)/shard_map/psum | solution.py:12
  384.5 5.1 copy-start.2
  537.7 6.7 copy-start.1
  730.9 11.4 %slice-start = ((f32[1024,1024]{0,1:T(8,128)}), f32[1024,128]{0,1:T(8,128)S(1)}, s32[]{:S(2)}) async-start(f32[1024,1024]{0,1:T(8,128)} %all-reduce.7.cloned.1.call-done), calls=%async_computation.5 | async-start | bytes 1048576 | tf_op jit(solution)/shard_map/slice | solution.py:27
  733.6 33.7 %copy-start = (f32[192,1024]{1,0:T(8,128)}, f32[192,1024]{1,0:T(8,128)S(1)}, u32[]{:S(2)}) copy-start(f32[192,1024]{1,0:T(8,128)S(1)} %fusion.26) | copy-start | bytes 2359300
Sparse Core Ops, SparseCore 0:
  19.5 132.3 all-reduce.4
  182.9 98.4 reduce-scatter.3
  283.7 87.8 all-gather.1
  384.6 128.3 all-reduce.6
where the time goes:
time: 783 us; the launch traced here: 775 us
  waiting for transfers between devices  444 us (57%)
  other arithmetic  211 us (27%)
  matrix products  74.5 us (10%)
  local copies, waits for them, and re-layouts  31.6 us (4%)
  between operations  14.1 us (2%)
    psum x2, waiting for transfers between devices, spread(): return lax.psum(block, axis)  255 us
    another operation x24, other arithmetic, left_looking(): diag_factor = jnp.linalg.cholesky(update_top[offset:offset + BLOCK])  99.8 us
    reduce_scatter x1, waiting for transfers between devices, local(): lax.psum_scatter(partial_value, 'obs', scatter_dimension=0, tiled=True)  98.6 us
    all_gather x1, waiting for transfers between devices, local(): gathered = lax.all_gather(owned_rows, 'obs', axis=0, tiled=True)  90.1 us
    another operation x16, other arithmetic, apply_lower(): lax.linalg.triangular_solve(diag_factor, values, left_side=False, lower=T...  84 us
    dot_general x7, matrix products, left_looking(): jnp.dot(factor_top[:, :offset], earlier.T, precision=lax.Precision.HIGHES...  26.8 us
    dot_general x1, matrix products, local(): lax.dot_general(design, weighted, (((0,), (0,)), ((), ())), precision=lax...  24.3 us
    unnamed x18, local copies, waits for them, and re-layouts  17.9 us
  transfers between devices with their start and end apart: 4, of which 4 were waited for; matrix products, arithmetic and copies ran while one was open for 1% of the time, Pallas kernels for 0%

commit v1 on v0

--- a/solution.py
+++ b/solution.py
@@ -9,7 +9,12 @@
 
 def spread(block, axis, holder):
     block = jnp.where(lax.axis_index(axis) == holder, block, jnp.zeros_like(block))
-    return lax.psum(block, axis)
+
+    def pass_floor(frame):
+        v_now = lax.all_gather(frame, axis_name=axis)
+        return jnp.sum(v_now, axis=0)
+
+    return pass_floor(block)
 
 
 def apply_lower(diag_factor, values):

time: 783 us -> 1230 us (1.57)
  waiting for transfers between devices: 444 us -> 842 us
  other arithmetic: 211 us -> 264 us
    all_gather x0 -> x2, waiting for transfers between devices: none -> 652 us  [pass_floor(): v_now = lax.all_gather(frame, axis_name=axis)]
    psum x2 -> x0, waiting for transfers between devices: 255 us -> none  [spread(): return lax.psum(block, axis)]
    reduce_sum x0 -> x2, other arithmetic: none -> 46.3 us  [pass_floor(): return jnp.sum(v_now, axis=0)]
  transfers between devices with their start and end apart: 4 -> 4, of which waited for: 4 -> 4; matrix products, arithmetic and copies ran while one was open for 1% -> 0% of each run, Pallas kernels for 0% -> 0%
where the time goes in v1:
time: 1230 us; the launch traced here: 1220 us
  waiting for transfers between devices  842 us (68%)
  other arithmetic  264 us (21%)
  matrix products  75.6 us (6%)
  local copies, waits for them, and re-layouts  27.5 us (2%)
  between operations  14 us (1%)
    all_gather x2, waiting for transfers between devices, pass_floor(): v_now = lax.all_gather(frame, axis_name=axis)  652 us
    another operation x24, other arithmetic, left_looking(): diag_factor = jnp.linalg.cholesky(update_top[offset:offset + BLOCK])  99.6 us
    reduce_scatter x1, waiting for transfers between devices, local(): lax.psum_scatter(partial_value, 'obs', scatter_dimension=0, tiled=True)  99.1 us
    all_gather x1, waiting for transfers between devices, local(): gathered = lax.all_gather(owned_rows, 'obs', axis=0, tiled=True)  90.2 us
    another operation x16, other arithmetic, apply_lower(): lax.linalg.triangular_solve(diag_factor, values, left_side=False, lower=T...  84.4 us
    reduce_sum x2, other arithmetic, pass_floor(): return jnp.sum(v_now, axis=0)  46.3 us
    dot_general x7, matrix products, left_looking(): jnp.dot(factor_top[:, :offset], earlier.T, precision=lax.Precision.HIGHES...  26.5 us
  transfers between devices with their start and end apart: 4, of which 4 were waited for; matrix products, arithmetic and copies ran while one was open for 0% of the time, Pallas kernels for 0%

profile of v1, /device:TPU:7, one launch (start us, length us, event | category | flops | bytes accessed | tf_op | source)
XLA Modules:
  0.0 1223.2 jit_solution(13630293304010560138)
XLA Ops:
  6.5 5.0 slice_select_fusion.1
  11.6 330.8 %all-gather.8.cloned.1.call-done = f32[16384,1024]{1,0:T(8,128)} async-done(((f32[1024,1024]{1,0:T(8,128)}), f32[16384,1024]{1,0:T(8,128)}) %all-gather.8.cloned.1.call-update) | async-done | bytes 67108880 | tf_op jit(solution)/shard_map/all_gather | solution.py:14
  342.4 22.9 %reduce_sum.18 = f32[1024,1024]{1,0:T(8,128)} reduce(f32[16,1024,1024]{2,1,0:T(8,128)} %bitcast, f32[]{:T(128)} %constant.415.clone.1), dimensions={0}, to_apply=%region_1.2 | reduce | flops 15728640 | bytes 71303168 | tf_op jit(solution)/shard_map/reduce_sum | solution.py:15
  365.3 5.4 copy.77
  370.7 24.3 %convolution_bitcast_fusion = f32[1536,1024]{0,1:T(8,128)} fusion(f32[1024,1536]{1,0:T(8,128)} %param.35, f32[1024,1024]{0,1:T(8,128)} %copy.77, f32[1024]{0:T(1024)S(1)} %copy-done.11), kind=kOutput, calls=%fused_computation | convolution fusion | flops 19328401408 | bytes 16781312 | tf_op jit(solution)/shard_map/dot_general | solution.py:63
  395.0 6.5 copy.75
  401.6 99.1 %reduce-scatter.4.cloned.1.call-done = f32[192,1024]{1,0:T(8,128)} async-done(((f32[1536,1024]{1,0:T(8,128)}), f32[192,1024]{1,0:T(8,128)}) %reduce-scatter.4.cloned.1.call-update) | async-done | bytes 786448 | tf_op jit(solution)/shard_map/reduce_scatter | solution.py:70
  500.8 90.2 %all-gather.6.cloned.1.call-done = f32[1536,1024]{1,0:T(8,128)} async-done(((f32[192,1024]{1,0:T(8,128)}), f32[1536,1024]{1,0:T(8,128)}) %all-gather.6.cloned.1.call-update) | async-done | bytes 6291472 | tf_op jit(solution)/shard_map/all_gather | solution.py:71
  590.9 5.0 slice_select_fusion
  601.3 321.6 %all-gather.10.cloned.1.call-done = f32[16384,1024]{1,0:T(8,128)} async-done(((f32[1024,1024]{1,0:T(8,128)}), f32[16384,1024]{1,0:T(8,128)}) %all-gather.10.cloned.1.call-update) | async-done | bytes 67108880 | tf_op jit(solution)/shard_map/all_gather | solution.py:14
  922.8 23.4 %reduce_sum.19 = f32[1024,1024]{1,0:T(8,128)} reduce(f32[16,1024,1024]{2,1,0:T(8,128)} %bitcast.2, f32[]{:T(128)} %constant.415.clone.1), dimensions={0}, to_apply=%region_3.4 | reduce | flops 15728640 | bytes 71303168 | tf_op jit(solution)/shard_map/reduce_sum | solution.py:15
  951.7 11.7 cholesky.134
  964.7 9.8 custom-call.40
  982.7 11.7 cholesky.145
  995.7 9.9 custom-call.41
  1012.8 11.7 cholesky.156
  1026.5 9.8 custom-call.42
  1048.8 3.4 fusion.15
  1053.9 11.7 cholesky.167
  1066.8 9.8 custom-call.43
  1084.1 4.0 fusion.21
  1088.3 12.1 cholesky.178
  1101.7 9.8 custom-call.44
  1117.4 4.6 fusion.18
  1122.1 11.9 cholesky.189
  1135.3 9.8 custom-call.45
  1150.7 5.3 fusion.12
  1156.2 11.7 cholesky.200
  1169.2 10.0 custom-call.46
  1184.7 6.0 fusion.1
  1191.0 11.7 cholesky.211
  1204.0 9.8 custom-call.47
  (139 shorter events, 78.9 us)
Async XLA Ops:
  6.5 335.9 %all-gather.8.cloned.1.call-start = ((), (), s32[]{:S(2)}) async-start(), calls=%async_computation.2 | async-start | bytes 71303168 | tf_op jit(solution)/shard_map/all_gather | solution.py:14
  11.5 489.1 %reduce-scatter.4.cloned.1.call-start = ((), (), s32[]{:S(2)}) async-start(), calls=%async_computation.4 | async-start | bytes 7077888 | tf_op jit(solution)/shard_map/reduce_scatter | solution.py:70
  365.3 5.4 copy-start.11
  401.6 189.3 %all-gather.6.cloned.1.call-start = ((), (), s32[]{:S(2)}) async-start(), calls=%async_computation.1 | async-start | bytes 7077888 | tf_op jit(solution)/shard_map/all_gather | solution.py:71
  500.7 422.1 %all-gather.10.cloned.1.call-start = ((), (), s32[]{:S(2)}) async-start(), calls=%async_computation.3 | async-start | bytes 71303168 | tf_op jit(solution)/shard_map/all_gather | solution.py:14
  974.5 2.6 copy-start.9
  977.1 3.2 copy-start.4
  980.3 56.7 %copy-start.1 = (f32[192,1024]{1,0:T(8,128)S(1)}, f32[192,1024]{1,0:T(8,128)}, u32[]{:S(2)}) copy-start(f32[192,1024]{1,0:T(8,128)} %reduce-scatter.4.cloned.1.call-done) | copy-start | bytes 2359300
  980.3 56.7 %copy-start.10 = (f32[1,128,128]{1,2,0:T(8,128)S(1)}, f32[1,128,128]{1,2,0:T(8,128)}, u32[]{:S(2)}) copy-start(f32[1,128,128]{1,2,0:T(8,128)} %copy-done.9) | copy-start | bytes 196612
  980.9 0.8 copy-start.3
  1005.6 7.0 copy-start.8
  1037.9 0.6 copy-start.6
  1041.8 36.4 %copy-start.2 = (f32[1024,128]{1,0:T(8,128)S(1)}, f32[1024,128]{1,0:T(8,128)}, u32[]{:S(2)}) copy-start(f32[1024,128]{1,0:T(8,128)} %get-tuple-element.205) | copy-start | bytes 1572868
  1052.1 0.8 copy-start.5
  1156.0 34.7 %copy-start.7 = (f32[128,128]{1,0:T(8,128)S(1)}, f32[128,128]{1,0:T(8,128)}, u32[]{:S(2)}) copy-start(f32[128,128]{1,0:T(8,128)} %get-tuple-element.201) | copy-start | bytes 196612
  1182.0 33.6 %copy-start = (f32[192,1024]{1,0:T(8,128)}, f32[192,1024]{1,0:T(8,128)S(1)}, u32[]{:S(2)}) copy-start(f32[192,1024]{1,0:T(8,128)S(1)} %fusion.26) | copy-start | bytes 2359300
Sparse Core Ops, SparseCore 0:
  11.7 330.6 all-gather.7
  401.7 98.9 reduce-scatter.3
  503.0 87.8 all-gather.5
  596.0 326.7 all-gather.9
